TPU v7x, 512 devices: a whole 4x8x8 slice. The times are simulated.
512 devices in a mesh: wide: 32 (over y, z_hi), narrow: 16 (over z_lo, x, core).
Axes of the slice: x: 4, y: 8, z: 8 (z_hi: 4, z_lo: 2; z = z_hi * 2 + z_lo), core: 2. Of those that a mesh axis runs over, the one named last changes fastest.
Arguments:
- daily_fields: bfloat16 [1024, 704, 1440], P('narrow', 'wide'), may hold values from -6 to 6
- order_table: int32 [384], replicated, may hold values from 0 to 383, as said below
- lag_days: int32 [3], replicated, may hold values from 1 to 8, as said below
- lag_weights: float32 [3, 384, 384, 2], P(None, 'narrow', 'wide'), may hold values from -0.5 to 0.5
Outputs:
- noise_variance: float32 [384, 384, 2], P('narrow', 'wide')
- covariance_panel: float32 [384, 48, 6144], P('wide', None, 'narrow')
Inputs may be any that keep to these rules, and one draw needn't show every extreme that they name: `order_table`: slots 2k and 2k+1 hold the two orders m and 383 - m of one pair, the even one in slot 2k; every order appears once. `lag_days`: three different lags; one of them is 8.
All inputs are finite; a program needn't handle non-finite values.
Results may differ from a plain program's by a relative error of at most 0.0087.
Values may be sent and summed in bfloat16 or wider, within the bound.
A program may use at most 64 MiB of HBM per device.

v0:
```python
import math

import jax
import jax.numpy as jnp
from jax import lax
from jax.sharding import PartitionSpec as P

NLAT = 704
NLON = 1440
M = 384
L = 384
LAGMAX = 8
ROW_DEG = 3


def dft_table(order_table):
    longitude = jnp.arange(NLON, dtype=jnp.int32)
    phase_turns = order_table[:, None] * longitude[None, :] % NLON
    angle = phase_turns.astype(jnp.float32) * (2.0 * math.pi / NLON)
    norm_scale = 1.0 / math.sqrt(NLON)
    return jnp.stack([jnp.cos(angle) * norm_scale, -jnp.sin(angle) * norm_scale], axis=1).astype(
        jnp.bfloat16
    )


def lat_basis():
    degree = jnp.arange(L, dtype=jnp.int32)
    odd_lat = 2 * jnp.arange(NLAT, dtype=jnp.int32) + 1
    period = 4 * NLAT
    even_turns = degree[:, None] * odd_lat[None, :] % period
    odd_turns = (degree[:, None] + 1) * odd_lat[None, :] % period
    angle_unit = math.pi / (2 * NLAT)
    norm_scale = math.sqrt(2.0 / NLAT)
    cosines = jnp.cos(even_turns.astype(jnp.float32) * angle_unit) * norm_scale
    sines = jnp.sin(odd_turns.astype(jnp.float32) * angle_unit) * norm_scale
    return jnp.stack([cosines, sines]).astype(jnp.bfloat16)


def body(daily_fields, order_table, lag_days, lag_weights):
    wide_count = lax.axis_size("wide")
    narrow_count = lax.axis_size("narrow")
    days_local, lat_local, lon_count = daily_fields.shape
    slot_local = M // wide_count
    pair_local = slot_local // 2
    deg_local = L // narrow_count
    times_all = days_local * narrow_count
    kept_days = times_all - LAGMAX
    dft_rows = dft_table(order_table).reshape(M * 2, lon_count)
    spectra = lax.dot_general(
        dft_rows, daily_fields, (((1,), (2,)), ((), ())), preferred_element_type=jnp.float32
    )
    spectra = spectra.astype(jnp.bfloat16).reshape(M // 2, 4, days_local * lat_local)
    received = lax.all_to_all(spectra, "wide", split_axis=0, concat_axis=0, tiled=True)
    received = received.reshape(wide_count, pair_local, 2, 2, days_local, lat_local)
    lat_table = lat_basis().reshape(2, L, wide_count, lat_local)
    coeffs = lax.dot_general(
        lat_table, received, (((2, 3), (0, 5)), ((0,), (2,))), preferred_element_type=jnp.float32
    )
    coeffs = coeffs.astype(jnp.bfloat16)
    packed = coeffs.reshape(2, L, pair_local, 2 * days_local)
    regrouped = lax.all_to_all(packed, "narrow", split_axis=1, concat_axis=0, tiled=True)
    series = regrouped.reshape(narrow_count, 2, deg_local, pair_local, 2, days_local)
    weights = jnp.transpose(lag_weights.reshape(3, deg_local, pair_local, 2, 2), (0, 3, 1, 2, 4))
    earlier = jnp.concatenate([jnp.zeros_like(series[:1]), series[:-1]], axis=0)
    joined = jnp.concatenate([earlier, series], axis=5)
    residual = series.astype(jnp.float32)
    for position in range(3):
        shifted = lax.dynamic_slice_in_dim(
            joined, days_local - lag_days[position], days_local, axis=5
        )
        residual = residual - weights[position][None, :, :, :, :, None] * shifted.astype(
            jnp.float32
        )
    day_index = (
        jnp.arange(narrow_count, dtype=jnp.int32)[:, None] * days_local
        + jnp.arange(days_local, dtype=jnp.int32)[None, :]
    )
    residual = jnp.where((day_index >= LAGMAX)[:, None, None, None, None, :], residual, 0.0)
    spread = jnp.sum(residual * residual, axis=(0, 5)) / kept_days
    noise_variance = jnp.transpose(spread, (1, 2, 0, 3)).reshape(deg_local, slot_local, 2)
    rounded = residual.astype(jnp.bfloat16)
    row_part = jnp.transpose(rounded[:, :, :ROW_DEG, :, 0, :], (3, 1, 2, 0, 4)).reshape(
        slot_local, ROW_DEG, times_all
    )
    row_series = lax.all_gather(row_part, "narrow", axis=1, tiled=True)
    column_part = jnp.transpose(rounded[:, :, ROW_DEG, :, 0, :], (2, 1, 0, 3)).reshape(
        slot_local, times_all
    )
    cov_panel = lax.dot_general(
        row_series,
        lax.all_gather(column_part, "wide", axis=0, tiled=True),
        (((2,), (1,)), ((), ())),
        preferred_element_type=jnp.float32,
    )
    cov_panel = cov_panel / math.sqrt(kept_days)
    return (noise_variance, cov_panel)


def solution(mesh):
    placed = (P("narrow", "wide", None), P(), P(), P(None, "narrow", "wide", None))
    return jax.shard_map(
        body,
        mesh=mesh,
        in_specs=placed,
        out_specs=(P("narrow", "wide", None), P("wide", None, "narrow")),
        check_vma=False,
    )
```

profile of v0, /device:TPU:32, one launch (start us, length us, event | category | flops | bytes accessed | tf_op | source)
XLA Modules:
  0.0 365.0 jit_solution(9568581418225816928)
XLA Ops:
  7.2 10.3 %multiply_convert_fusion.1 = (bf16[384,1,1440]{0,2,1:T(8,128)(2,1)S(1)}, bf16[384,1,1440]{0,2,1:T(8,128)(2,1)S(1)}) fusion(s32[384]{0:T(512)} %param.5), kind=kLoop, calls=%fused_computation.12 | loop fusion | flops 7741440 | bytes 2213376 | tf_op jit(solution)/shard_map/convert
  17.5 1.6 pad_maximum_fusion
  19.1 5.9 %copy.73 = bf16[384,2,1440]{2,1,0:T(2,128)(2,1)S(1)} copy(bf16[384,2,1440]{0,2,1:T(8,128)(2,1)} %pad_maximum_fusion) | data formatting | bytes 4423680 | tf_op jit(solution)/shard_map/stack | solution.py:21
  25.0 2.9 convert_element_type.67
  27.9 6.5 %fusion.8 = bf16[768,64,22]{0,1,2:T(8,128)(2,1)S(1)} fusion(bf16[64,22,1440]{2,0,1:T(8,128)(2,1)} %param.4, bf16[768,1440]{1,0:T(8,128)(2,1)} %convert_element_type.67), kind=kOutput, calls=%fused_computation.17 | convolution fusion | flops 3115352064 | bytes 8429568 | tf_op jit(solution)/shard_map/dot_general | solution.py:49
  34.4 20.2 %copy.75 = bf16[768,64,22]{2,1,0:T(8,128)(2,1)} copy(bf16[768,64,22]{0,1,2:T(8,128)(2,1)S(1)} %fusion.8) | data formatting | bytes 4325376 | tf_op jit(solution)/shard_map/convert_element_type | solution.py:52
  54.7 21.1 %reshape.289 = bf16[192,4,1408]{2,1,0:T(4,128)(2,1)} reshape(bf16[768,64,22]{2,1,0:T(8,128)(2,1)} %copy.75) | data formatting | bytes 4325376 | tf_op jit(solution)/shard_map/reshape | solution.py:52
  75.8 15.8 %all-to-all-start = ((bf16[192,4,1408]{2,1,0:T(4,128)(2,1)}), bf16[192,4,1408]{2,1,0:T(4,128)(2,1)S(1)}, u32[]{:S(2)}, u32[]{:S(2)}) async-start(bf16[192,4,1408]{2,1,0:T(4,128)(2,1)} %reshape.289), calls=%async_computation | async-start | bytes 4325376 | tf_op jit(solution)/shard_map/all_to_all | solution.py:53
  91.6 8.7 %fusion.16 = (bf16[1,384,32,22]{1,2,3,0:T(8,128)(2,1)S(1)}, bf16[1,384,32,22]{1,2,3,0:T(8,128)(2,1)S(1)}) fusion(s32[32,22]{0,1:T(8,128)S(1)} %multiply_add_fusion, s32[384]{0:T(512)S(1)} %iota_add_fusion), kind=kLoop, calls=%fused_computation.26 | loop fusion | flops 5947392 | bytes 1085696 | tf_op jit(solution)/shard_map/convert.2
  100.3 55.5 %all-to-all-done = bf16[192,4,1408]{2,1,0:T(4,128)(2,1)S(1)} async-done(((bf16[192,4,1408]{2,1,0:T(4,128)(2,1)}), bf16[192,4,1408]{2,1,0:T(4,128)(2,1)S(1)}, u32[]{:S(2)}, u32[]{:S(2)}) %all-to-all-start) | async-done | bytes 2162720 | tf_op jit(solution)/shard_map/all_to_all | solution.py:53
  155.8 32.5 %reshape.304 = bf16[32,6,2,2,64,22]{5,4,3,2,1,0:T(8,128)(2,1)} reshape(bf16[192,4,1408]{2,1,0:T(4,128)(2,1)S(1)} %all-to-all-done) | data formatting | bytes 4325376 | tf_op jit(solution)/shard_map/reshape | solution.py:54
  188.3 13.7 %copy.77 = bf16[32,6,2,2,64,22]{4,0,5,3,1,2:T(8,128)(2,1)} copy(bf16[32,6,2,2,64,22]{5,4,3,2,1,0:T(8,128)(2,1)} %reshape.304) | data formatting | bytes 4325376 | tf_op jit(solution)/shard_map/reshape | solution.py:54
  202.0 3.8 %bitcast_convert_fusion = bf16[2,384,6,2,64]{1,4,3,2,0:T(8,128)(2,1)S(1)} fusion(bf16[32,6,2,2,64,22]{4,0,5,3,1,2:T(8,128)(2,1)} %copy.77, bf16[1,384,32,22]{1,2,3,0:T(8,128)(2,1)S(1)} %get-tuple-element.8, bf16[1,384,32,22]{1,2,3,0:T(8,128)(2,1)S(1)} %get-tuple-element.7), kind=kOutput, calls=%fused_computation.5 | convolution fusion | flops 833224704 | bytes 4423680 | tf_op jit(solution)/shard_map/dot_general | solution.py:56
  205.8 2.9 copy.78
  208.7 3.7 %all-to-all-start.1 = ((bf16[2,384,6,128]{3,0,2,1:T(2,128)(2,1)}), bf16[2,384,6,128]{3,0,2,1:T(2,128)(2,1)S(1)}, u32[]{:S(2)}, u32[]{:S(2)}) async-start(bf16[2,384,6,128]{3,0,2,1:T(2,128)(2,1)} %copy.78), calls=%async_computation.1 | async-start | bytes 2359296 | tf_op jit(solution)/shard_map/all_to_all | solution.py:61
  218.3 12.0 %all-to-all-done.1 = bf16[2,384,6,128]{3,0,2,1:T(2,128)(2,1)S(1)} async-done(((bf16[2,384,6,128]{3,0,2,1:T(2,128)(2,1)}), bf16[2,384,6,128]{3,0,2,1:T(2,128)(2,1)S(1)}, u32[]{:S(2)}, u32[]{:S(2)}) %all-to-all-start.1) | async-done | bytes 1179680 | tf_op jit(solution)/shard_map/all_to_all | solution.py:61
  233.0 1.4 copy.82
  234.5 2.4 slice.32
  236.9 8.3 %fusion = bf16[16,2,24,6,2,128]{5,4,2,3,1,0:T(2,128)(2,1)S(1)} fusion(bf16[15,2,24,6,2,64]{5,4,2,3,1,0:T(2,128)(2,1)} %slice.32, bf16[16,2,24,6,2,64]{5,4,2,3,1,0:T(2,128)(2,1)S(1)} %reshape.292), kind=kLoop, calls=%fused_computation.4 | loop fusion | flops 7077888 | bytes 4644864 | tf_op jit(solution)/shard_map/concatenate | solution.py:65
  245.2 13.9 %fusion.31 = (bf16[16,2,24,6,2,64]{5,4,2,3,1,0:T(2,128)(2,1)S(1)}, f32[16,2,24,6,2,64]{5,4,2,3,1,0:T(2,128)}) fusion(bf16[16,2,24,6,2,128]{5,4,2,3,1,0:T(2,128)(2,1)S(1)} %fusion, s32[]{:T(128)S(6)} %select_n.62, f32[2,24,6,2]{3,1,2,0:T(8,128)S(1)} %copy-done.2, s32[]{:T(128)S(6)} %select_n.61, f32[2,24,6,2]{3,1,2,0:T(8,128)S(1)} %copy-done.3, ...), kind=kLoop, calls=%fused_computation.54 | loop fusion | flops 7077888 | bytes 8265484 | tf_op jit(solution)/shard_map/convert_element_type | solution.py:81
  259.1 1.4 copy-done
  262.7 86.4 %all-gather = bf16[32,12,1024]{2,1,0:T(8,128)(2,1)S(1)} all-gather(bf16[1,12,1024]{2,1,0:T(8,128)(2,1)S(1)} %reshape.297), channel_id=1, replica_groups=mesh['wide'=32,'narrow'=16] {'wide'}, dimensions={0}, use_global_device_ids=true | all-gather | bytes 811008 | tf_op jit(solution)/shard_map/all_gather | solution.py:91
  349.3 4.9 %multiply_reduce_fusion = f32[2,24,6,2]{3,1,2,0:T(8,128)S(1)} fusion(f32[16,2,24,6,2,64]{5,4,2,3,1,0:T(2,128)} %get-tuple-element.3), kind=kLoop, calls=%fused_computation.1 | loop fusion | flops 1179072 | bytes 2361600 | tf_op jit(solution)/shard_map/reduce_sum | solution.py:79
  355.0 3.2 convolution_multiply_fusion
  (34 shorter events, 7.7 us)
Async XLA Ops:
  75.8 80.0 %all-to-all-start = ((bf16[192,4,1408]{2,1,0:T(4,128)(2,1)}), bf16[192,4,1408]{2,1,0:T(4,128)(2,1)S(1)}, u32[]{:S(2)}, u32[]{:S(2)}) async-start(bf16[192,4,1408]{2,1,0:T(4,128)(2,1)} %reshape.289), calls=%async_computation | async-start | bytes 4325376 | tf_op jit(solution)/shard_map/all_to_all | solution.py:53
  205.8 6.9 %copy-start.5 = (s32[3]{0:T(128)S(1)}, s32[3]{0:T(128)}, u32[]{:S(2)}) copy-start(s32[3]{0:T(128)} %param.6) | copy-start | bytes 40
  205.8 11.4 %copy-start.4 = (f32[3,24,12,2]{1,3,2,0:T(2,128)S(1)}, f32[3,24,12,2]{1,3,2,0:T(2,128)}, u32[]{:S(2)}) copy-start(f32[3,24,12,2]{1,3,2,0:T(2,128)} %param.7) | copy-start | bytes 20740
  208.7 21.7 %all-to-all-start.1 = ((bf16[2,384,6,128]{3,0,2,1:T(2,128)(2,1)}), bf16[2,384,6,128]{3,0,2,1:T(2,128)(2,1)S(1)}, u32[]{:S(2)}, u32[]{:S(2)}) async-start(bf16[2,384,6,128]{3,0,2,1:T(2,128)(2,1)} %copy.78), calls=%async_computation.1 | async-start | bytes 2359296 | tf_op jit(solution)/shard_map/all_to_all | solution.py:61
  212.4 142.6 %all-gather.3.cloned.1.call-start = ((), (), s32[]{:S(2)}) async-start(), calls=%async_computation.2 | async-start | bytes 1671168 | tf_op jit(solution)/shard_map/all_gather | solution.py:85
  236.9 8.3 %copy-start.1 = (f32[2,24,6,2]{3,1,2,0:T(8,128)S(1)}, f32[2,24,6,2]{3,1,2,0:T(8,128)}, u32[]{:S(2)}) copy-start(f32[2,24,6,2]{3,1,2,0:T(8,128)} %get-tuple-element.4) | copy-start | bytes 6916
  236.9 8.3 %copy-start.2 = (f32[2,24,6,2]{3,1,2,0:T(8,128)S(1)}, f32[2,24,6,2]{3,1,2,0:T(8,128)}, u32[]{:S(2)}) copy-start(f32[2,24,6,2]{3,1,2,0:T(8,128)} %get-tuple-element.5) | copy-start | bytes 6916
  236.9 8.3 %copy-start.3 = (f32[2,24,6,2]{3,1,2,0:T(8,128)S(1)}, f32[2,24,6,2]{3,1,2,0:T(8,128)}, u32[]{:S(2)}) copy-start(f32[2,24,6,2]{3,1,2,0:T(8,128)} %get-tuple-element.6) | copy-start | bytes 6916
  259.1 1.4 copy-start
Sparse Core Ops, SparseCore 0:
  261.7 35.1 all-gather.2
where the time goes:
time: 366 us; the launch traced here: 365 us
  local copies, waits for them, and re-layouts  112 us (31%)
  blocking collectives  86.4 us (24%)
  waiting for transfers between devices  67.6 us (18%)
  other arithmetic  47.8 us (13%)
  starting transfers between devices  19.8 us (5%)
  between operations  18.1 us (5%)
  matrix products  13.5 us (4%)
    all_gather x1, blocking collectives, body(): lax.all_gather(column_part, 'wide', axis=0, tiled=True)  86.4 us
    all_to_all x1, waiting for transfers between devices, body(): lax.all_to_all(spectra, 'wide', split_axis=0, concat_axis=0, tiled=True)  55.5 us
    reshape x2, local copies, waits for them, and re-layouts, body(): received.reshape(wide_count, pair_local, 2, 2, days_local, lat_local)  46.2 us
    reshape x1, local copies, waits for them, and re-layouts, body(): spectra.astype(jnp.bfloat16).reshape(M // 2, 4, days_local * lat_local)  21.1 us
    convert_element_type x1, local copies, waits for them, and re-layouts, body(): spectra.astype(jnp.bfloat16).reshape(M // 2, 4, days_local * lat_local)  20.2 us
    another operation x2, other arithmetic  19 us
    all_to_all x1, starting transfers between devices, body(): lax.all_to_all(spectra, 'wide', split_axis=0, concat_axis=0, tiled=True)  15.8 us
    convert_element_type x1, other arithmetic, body(): rounded = residual.astype(jnp.bfloat16)  13.9 us
  transfers between devices with their start and end apart: 3, of which 2 were waited for; matrix products, arithmetic and copies ran while one was open for 5% of the time, Pallas kernels for 0%

commit v1 on v0

v1 whole, which is shorter than its diff:
```python
import math

import jax
import jax.numpy as jnp
import numpy as np
from jax import lax
from jax.experimental import pallas as pl
from jax.experimental.pallas import tpu as pltpu
from jax.sharding import PartitionSpec as P

NLAT = 704
NLON = 1440
M = 384
L = 384
LAGMAX = 8
ROW_DEG = 3
WIDE = 32
NARROW = 16
CH = 3
SLOTS = 4
ROWS = 24
LANES = 128
PAIRS = NARROW // 2

BF16 = jnp.bfloat16
F32 = jnp.float32
MESH = pl.DeviceIdType.MESH

WIDE_OFFS = sorted(
    [(a, b) for a in range(8) for b in range(4) if (a, b) != (0, 0)],
    key=lambda p: (min(p[0], 8 - p[0]) + 2 * min(p[1], 4 - p[1]), p),
)
NARROW_OFFS = sorted(
    [(a, b, c) for a in range(2) for b in range(4) for c in range(2) if (a, b, c) != (0, 0, 0)],
    key=lambda p: (p[0] + min(p[1], 4 - p[1]), p),
)


def fourier_tables():
    order = np.arange(M)
    angle = (order[:, None] * np.arange(NLON)[None, :] % NLON) * (2.0 * math.pi / NLON)
    scale = 1.0 / math.sqrt(NLON)
    return np.stack([np.cos(angle) * scale, -np.sin(angle) * scale]).astype(np.float32)


def latitude_tables():
    degree = np.arange(L)
    odd = 2 * np.arange(NLAT) + 1
    unit = math.pi / (2 * NLAT)
    scale = math.sqrt(2.0 / NLAT)
    even_part = np.cos((degree[:, None] * odd[None, :] % (4 * NLAT)) * unit) * scale
    odd_part = np.sin(((degree[:, None] + 1) * odd[None, :] % (4 * NLAT)) * unit) * scale
    table = np.stack([even_part, odd_part]).reshape(2, L, WIDE, 11, 2)
    table = np.transpose(table, (0, 1, 2, 4, 3))
    table = np.pad(table, ((0, 0), (0, 0), (0, 0), (0, 0), (0, 1)))
    return table.reshape(2, L, WIDE * ROWS).astype(np.float32)


def wide_peer(me, off):
    y = lax.rem(lax.div(me, 4) + off[0], 8)
    z = lax.rem(lax.rem(me, 4) + off[1], 4)
    return y * 4 + z


def narrow_peer(me, off):
    z = lax.rem(lax.div(me, 8) + off[0], 2)
    x = lax.rem(lax.rem(lax.div(me, 2), 4) + off[1], 4)
    c = lax.rem(lax.rem(me, 2) + off[2], 2)
    return z * 8 + x * 2 + c


def kernel(
    order_ref, lag_ref, weight_ref, fourier_ref, lat_ref, x_ref,
    var_ref, panel_ref,
    table, wave, spec_out, spec_in, coef_out, coef_in, wexp, series,
    row_out, row_in, col_out, col_in, rows32, cols32, colmat,
    s_spec, r_spec, s_coef, r_coef, s_row, r_row, s_col, r_col, local,
):
    w = lax.axis_index("wide")
    n = lax.axis_index("narrow")

    barrier = pltpu.get_barrier_semaphore()
    for off in WIDE_OFFS:
        pl.semaphore_signal(barrier, inc=1, device_id={"wide": wide_peer(w, off)}, device_id_type=MESH)
    for off in NARROW_OFFS:
        pl.semaphore_signal(barrier, inc=1, device_id={"narrow": narrow_peer(n, off)}, device_id_type=MESH)

    def send_wide(source, target, ch, s_sem, r_sem):
        return [
            pltpu.make_async_remote_copy(
                src_ref=source(wide_peer(w, off)), dst_ref=target, send_sem=s_sem.at[ch, i],
                recv_sem=r_sem.at[ch, i], device_id={"wide": wide_peer(w, off)}, device_id_type=MESH,
            )
            for i, off in enumerate(WIDE_OFFS)
        ]

    def send_narrow(source, target, ch, s_sem, r_sem):
        return [
            pltpu.make_async_remote_copy(
                src_ref=source(narrow_peer(n, off)), dst_ref=target, send_sem=s_sem.at[ch, i],
                recv_sem=r_sem.at[ch, i], device_id={"narrow": narrow_peer(n, off)}, device_id_type=MESH,
            )
            for i, off in enumerate(NARROW_OFFS)
        ]

    def launch(copies):
        for copy in copies:
            copy.start()
        return copies

    def arrive(copies):
        copies[0].wait()
        for copy in copies[1:]:
            copy.wait_recv()

    def drain(copies):
        for copy in copies[1:]:
            copy.wait_send()

    lane128 = lax.broadcasted_iota(jnp.int32, (ROWS, LANES), 1)
    left = lane128 < 64
    pads = jnp.zeros((256, LANES), F32)
    for slot in (11, 23, 35):
        wave[pl.ds(slot * 256, 256), :] = pads

    spectra = []
    for ch in range(CH):
        hot = (
            order_ref[pl.ds(ch * 128, 128), :] == lax.broadcasted_iota(jnp.int32, (128, M), 1)
        ).astype(F32).astype(BF16)
        for c in range(2):
            table[pl.ds(c * 128, 128), :] = jnp.dot(
                hot, fourier_ref[c], preferred_element_type=F32
            ).astype(BF16)
        for at, count in ((0, 4), (4, 4), (8, 4), (12, 4), (16, 4), (20, 2)):
            days = x_ref[pl.ds(at, count)].reshape(count * 64, NLON)
            out = lax.dot_general(
                table[...], days, (((1,), (1,)), ((), ())), preferred_element_type=F32
            )
            for half in range(count // 2):
                piece = out[:, half * 128 : (half + 1) * 128]
                slot = at // 2 + half
                wave[pl.ds(slot * 256, 256), :] = piece
                wave[pl.ds((24 + slot) * 256, 256), :] = piece
                wave[pl.ds((12 + slot) * 256, 256), :] = pltpu.roll(piece, 64, 1)

        def regroup(d, carry, ch=ch):
            for q in range(SLOTS):
                real = wave[pl.ds(d * 4 + q, ROWS, stride=256), :]
                imag = wave[pl.ds(12 * 256 + 128 + d * 4 + q, ROWS, stride=256), :]
                blk = jnp.where(left, real, imag)
                rows32[pl.ds(q * ROWS, ROWS), :] = blk
            spec_out[ch, d] = rows32[pl.ds(0, SLOTS * ROWS), :].astype(BF16)
            return carry

        lax.fori_loop(0, WIDE, regroup, 0)
        if ch == 0:
            pl.semaphore_wait(barrier, len(WIDE_OFFS) + len(NARROW_OFFS))
        spectra.append(
            launch(send_wide(lambda d, ch=ch: spec_out.at[ch, d], spec_in.at[ch, w], ch, s_spec, r_spec))
        )
        own = pltpu.make_async_copy(spec_out.at[ch, w], spec_in.at[ch, w], local.at[0, ch])
        own.start()
        spectra[-1].insert(0, own)

    coefs, row_copies, col_copies = [], [], []
    variance = jnp.zeros((2 * ROWS, LANES), F32)
    lane48 = lax.broadcasted_iota(jnp.int32, (2 * ROWS, LANES), 1)
    day = lax.rem(lane48, 64)
    left48 = lane48 < 64

    def latitude(ch):
        arrive(spectra[ch])
        parts = []
        for e in range(2):
            columns = []
            for q2 in range(2):
                at = (2 * q2 + e) * ROWS
                blk = spec_in[ch].astype(F32)[:, at : at + ROWS, :]
                columns.append(blk.reshape(WIDE * ROWS, LANES).astype(BF16))
            right = jnp.concatenate(columns, axis=1)
            parts.append(jnp.dot(lat_ref[e], right, preferred_element_type=F32))
        for m in range(NARROW):
            both = jnp.concatenate([parts[0][m * 24 : m * 24 + 24], parts[1][m * 24 : m * 24 + 24]], axis=0)
            coef_out[ch, m] = both.astype(BF16)
        copies = launch(
            send_narrow(lambda m: coef_out.at[ch, m], coef_in.at[ch, n], ch, s_coef, r_coef)
        )
        own = pltpu.make_async_copy(coef_out.at[ch, n], coef_in.at[ch, n], local.at[1, ch])
        own.start()
        copies.insert(0, own)
        coefs.append(copies)

    def residuals(ch, variance):
        arrive(coefs[ch])
        for q2 in range(2):
            k = 2 * ch + q2
            for i in range(3):
                re = jnp.broadcast_to(weight_ref[i, :, 2 * k : 2 * k + 1], (2 * ROWS, LANES))
                im = jnp.broadcast_to(weight_ref[i, :, 2 * k + 1 : 2 * k + 2], (2 * ROWS, LANES))
                wexp[i] = jnp.where(left48, re, im)
            before = jnp.zeros((2 * ROWS, LANES), F32)
            total = jnp.zeros((2 * ROWS, LANES), F32)
            held = None
            for m in range(NARROW):
                now = coef_in[ch, m, :, q2 * LANES : (q2 + 1) * LANES].astype(F32)
                res = now
                for i in range(3):
                    lag = lag_ref[i]
                    mixed = jnp.where(day >= 64 - lag, before, now)
                    res = res - wexp[i] * pltpu.roll(mixed, lag, 1)
                if m == 0:
                    res = jnp.where(day >= LAGMAX, res, 0.0)
                total = total + res * res
                before = pltpu.roll(now, 64, 1)
                for e in range(2):
                    top = res[e * ROWS : e * ROWS + 8]
                    if m % 2 == 0:
                        held = (held or []) + [top] if e == 1 else [top]
                    else:
                        both = jnp.where(left[:8], held[e], pltpu.roll(top, 64, 1))
                        series[pl.ds((2 * q2 + e) * 64 + (m // 2) * 8, 8), :] = both
            re = jnp.sum(jnp.where(left48, total, 0.0), axis=1, keepdims=True)
            im = jnp.sum(jnp.where(left48, 0.0, total), axis=1, keepdims=True)
            variance = variance + jnp.where(lane48 == 2 * k, re, 0.0) + jnp.where(lane48 == 2 * k + 1, im, 0.0)
        parts = []
        for q in range(SLOTS):
            for l in range(ROW_DEG):
                parts.append(series[pl.ds(q * 64 + l, PAIRS, stride=8), :])
        row_out[ch] = jnp.concatenate(parts, axis=0).astype(BF16)
        parts = [series[pl.ds(q * 64 + ROW_DEG, PAIRS, stride=8), :] for q in range(SLOTS)]
        col_out[ch] = jnp.concatenate(parts, axis=0).astype(BF16)
        copies = launch(send_wide(lambda d: col_out.at[ch], col_in.at[ch, w], ch, s_col, r_col))
        own = pltpu.make_async_copy(col_out.at[ch], col_in.at[ch, w], local.at[2, ch])
        own.start()
        copies.insert(0, own)
        col_copies.append(copies)
        copies = launch(send_narrow(lambda d: row_out.at[ch], row_in.at[ch, n], ch, s_row, r_row))
        own = pltpu.make_async_copy(row_out.at[ch], row_in.at[ch, n], local.at[3, ch])
        own.start()
        copies.insert(0, own)
        row_copies.append(copies)
        return variance

    latitude(0)
    latitude(1)
    variance = residuals(0, variance)
    latitude(2)
    variance = residuals(1, variance)
    variance = residuals(2, variance)
    var_ref[...] = variance / (NARROW * 64 - LAGMAX)

    for ch in range(CH):
        arrive(col_copies[ch])
        for d in range(WIDE):
            cols32[pl.ds((d * 12 + ch * 4) * 8, 32), :] = col_in[ch, d].astype(F32)
    for p in range(PAIRS):
        colmat[:, p * LANES : (p + 1) * LANES] = cols32[pl.ds(p, M, stride=8), :].astype(BF16)
    for ch in range(CH):
        arrive(row_copies[ch])
        for m in range(NARROW):
            blk = row_in[ch, m].astype(F32)
            for q in range(SLOTS):
                rows32[pl.ds(q * 384 + m * 24, 24), :] = blk[q * 24 : q * 24 + 24]
        for q in range(SLOTS):
            pieces = [rows32[pl.ds(q * 384 + p, 48, stride=8), :] for p in range(PAIRS)]
            rows = jnp.concatenate(pieces, axis=1).astype(BF16)
            out = lax.dot_general(
                rows, colmat[...], (((1,), (1,)), ((), ())), preferred_element_type=F32
            )
            panel_ref[ch * SLOTS + q] = out / math.sqrt(NARROW * 64 - LAGMAX)

    for copies in spectra + coefs + row_copies + col_copies:
        drain(copies)


def body(daily_fields, order_table, lag_days, lag_weights):
    fourier = jnp.asarray(fourier_tables(), BF16)
    lat = jnp.asarray(latitude_tables(), BF16)
    x = jnp.transpose(daily_fields, (1, 0, 2))
    order = jnp.transpose(order_table.reshape(WIDE, CH, SLOTS), (1, 0, 2)).reshape(M, 1)
    weights = jnp.transpose(lag_weights.reshape(3, 24, 6, 2, 2), (0, 3, 1, 2, 4)).reshape(3, 48, 12)
    vmem = pl.BlockSpec(memory_space=pltpu.VMEM)
    dma = pltpu.SemaphoreType.DMA
    nw, nn = len(WIDE_OFFS), len(NARROW_OFFS)
    variance, panel = pl.pallas_call(
        kernel,
        out_shape=(
            jax.ShapeDtypeStruct((2 * ROWS, LANES), F32),
            jax.ShapeDtypeStruct((CH * SLOTS, ROW_DEG * NARROW, M), F32),
        ),
        in_specs=[vmem, pl.BlockSpec(memory_space=pltpu.SMEM), vmem, vmem, vmem, vmem],
        out_specs=(vmem, vmem),
        scratch_shapes=[
            pltpu.VMEM((256, NLON), BF16),
            pltpu.VMEM((36 * 256, LANES), F32),
            pltpu.VMEM((CH, WIDE, SLOTS * ROWS, LANES), BF16),
            pltpu.VMEM((CH, WIDE, SLOTS * ROWS, LANES), BF16),
            pltpu.VMEM((CH, NARROW, 48, 256), BF16),
            pltpu.VMEM((CH, NARROW, 48, 256), BF16),
            pltpu.VMEM((3, 48, LANES), F32),
            pltpu.VMEM((SLOTS * 64, LANES), F32),
            pltpu.VMEM((CH, 96, LANES), BF16),
            pltpu.VMEM((CH, NARROW, 96, LANES), BF16),
            pltpu.VMEM((CH, 32, LANES), BF16),
            pltpu.VMEM((CH, WIDE, 32, LANES), BF16),
            pltpu.VMEM((SLOTS * 384, LANES), F32),
            pltpu.VMEM((M * 8, LANES), F32),
            pltpu.VMEM((M, PAIRS * LANES), BF16),
            dma((CH, nw)), dma((CH, nw)), dma((CH, nn)), dma((CH, nn)),
            dma((CH, nn)), dma((CH, nn)), dma((CH, nw)), dma((CH, nw)), dma((4, CH)),
        ],
        compiler_params=pltpu.CompilerParams(
            collective_id=0, has_side_effects=True, vmem_limit_bytes=60 * 1024 * 1024
        ),
        name="sphere",
    )(order, lag_days, weights, fourier, lat, x)
    noise = jnp.transpose(variance[:, :12].reshape(2, 24, 6, 2), (1, 2, 0, 3)).reshape(24, 12, 2)
    return noise, panel


def solution(mesh):
    placed = (P("narrow", "wide", None), P(), P(), P(None, "narrow", "wide", None))
    return jax.shard_map(
        body,
        mesh=mesh,
        in_specs=placed,
        out_specs=(P("narrow", "wide", None), P("wide", None, "narrow")),
        check_vma=False,
    )
```

time: 366 us -> 135 us (0.37)
  the two profiles are of different devices: /device:TPU:32 before, /device:TPU:1 now
where the time goes in v1:
time: 135 us
  Pallas kernels  127 us (94%)
  local copies, waits for them, and re-layouts  6.83 us (5%)
    pallas_call x1, Pallas kernels, body(): pl.pallas_call(kernel, out_shape=(jax.ShapeDtypeStruct((2 * ROWS, LANES),...  127 us

profile of v1, /device:TPU:1, one launch (start us, length us, event | category | flops | bytes accessed | tf_op | source)
XLA Modules:
  0.0 134.6 jit_solution(13952423143704665508)
XLA Ops:
  0.6 0.8 copy.22
  1.4 0.1 reshape.25
  1.5 0.7 copy.18.weight_ref
  2.2 0.8 reshape.22
  3.1 0.8 reshape.28.order_ref
  3.8 127.1 %sphere.1 = (f32[48,128]{1,0:T(8,128)}, f32[12,48,384]{2,1,0:T(8,128)}) custom-call(s32[384,1]{1,0:T(8,128)} %reshape.28.order_ref, s32[3]{0:T(128)} %lag_ref.1, f32[3,48,12]{2,1,0:T(8,128)} %copy.18.weight_ref, bf16[2,384,1440]{2,1,0:T(8,128)(2,1)} %constant.4.clone.fourier_ref, bf16[2,384,768]{2,1,0:T(8,128)(2,1)} %constant.5.clone.lat_ref, ...), custom_call_target="tpu_custom_call" | custom-call | tf_op jit(solution)/shard_map/sphere/pallas_call | solution.py:286
  131.0 0.8 copy.19
  131.8 0.1 reshape.26
  131.9 0.6 copy.20
  132.5 2.1 %copy.24 = f32[12,48,384]{2,1,0:T(8,128)} copy(f32[12,48,384]{2,1,0:T(8,128)} %get-tuple-element.9) | data formatting | bytes 1769472
  (1 shorter events, 0.0 us)

commit v2 on v1

v2 whole, which is shorter than its diff:
```python
import math

import jax
import jax.numpy as jnp
import numpy as np
from jax import lax
from jax.experimental import pallas as pl
from jax.experimental.pallas import tpu as pltpu
from jax.sharding import PartitionSpec as P

NLAT = 704
NLON = 1440
M = 384
L = 384
LAGMAX = 8
ROW_DEG = 3
WIDE = 32
NARROW = 16
CH = 6
AHEAD = 2
ROWS = 24
LANES = 128
PAIRS = NARROW // 2
BAND = 2 * WIDE * 2

BF16 = jnp.bfloat16
F32 = jnp.float32
MESH = pl.DeviceIdType.MESH

Z_OFFS = [(0, 1), (0, 3), (0, 2)]
Y_OFFS = [(1, 0), (7, 0), (2, 0), (6, 0), (3, 0), (5, 0), (4, 0)]
ZLO_OFFS = [(1, 0, 0)]
XC_OFFS = [(0, 0, 1), (0, 1, 0), (0, 3, 0), (0, 1, 1), (0, 3, 1), (0, 2, 0), (0, 2, 1)]


def fourier_tables():
    order = np.arange(M)
    angle = (order[:, None] * np.arange(NLON)[None, :] % NLON) * (2.0 * math.pi / NLON)
    scale = 1.0 / math.sqrt(NLON)
    return np.stack([np.cos(angle) * scale, -np.sin(angle) * scale]).astype(np.float32)


def latitude_tables():
    degree = np.arange(L)
    odd = 2 * np.arange(NLAT) + 1
    unit = math.pi / (2 * NLAT)
    scale = math.sqrt(2.0 / NLAT)
    even_part = np.cos((degree[:, None] * odd[None, :] % (4 * NLAT)) * unit) * scale
    odd_part = np.sin(((degree[:, None] + 1) * odd[None, :] % (4 * NLAT)) * unit) * scale
    table = np.stack([even_part, odd_part]).reshape(2, L, WIDE, 11, 2)
    table = np.transpose(table, (0, 1, 2, 4, 3))
    table = np.pad(table, ((0, 0), (0, 0), (0, 0), (0, 0), (0, 1)))
    return table.reshape(2, L, WIDE * ROWS).astype(np.float32)


def wide_peer(me, off):
    y = lax.rem(lax.div(me, 4) + off[0], 8)
    z = lax.rem(lax.rem(me, 4) + off[1], 4)
    return y * 4 + z


def narrow_peer(me, off):
    z = lax.rem(lax.div(me, 8) + off[0], 2)
    x = lax.rem(lax.rem(lax.div(me, 2), 4) + off[1], 4)
    c = lax.rem(lax.rem(me, 2) + off[2], 2)
    return z * 8 + x * 2 + c


def wide_step(me, k):
    j = lax.div(k, 4)
    up = lax.div(j + 1, 2)
    dy = lax.rem(lax.rem(j, 2) * up + (1 - lax.rem(j, 2)) * (8 - up), 8)
    h = lax.rem(k, 4)
    dz = (h + 1 - lax.rem(h, 2)) * lax.div(h + 3, 4) * (1 - lax.div(h, 3)) + 2 * lax.div(h, 3)
    return wide_peer(me, (dy, dz))


def narrow_step(me, k):
    h = lax.div(k, 4)
    dx = (h + 1 - lax.rem(h, 2)) * lax.div(h + 3, 4) * (1 - lax.div(h, 3)) + 2 * lax.div(h, 3)
    return narrow_peer(me, (lax.rem(k, 2), dx, lax.rem(lax.div(k, 2), 2)))


def each(start, stop, act):
    def step(k, carry):
        act(k)
        return carry

    lax.fori_loop(start, stop, step, 0)


def kernel(
    order_ref, lag_ref, weight_ref, fourier_ref, lat_ref, x_ref,
    var_ref, panel_ref,
    table, wave, spec_out, spec_in, coef_out, coef_in, wexp, series,
    row_out, row_in, col_out, col_in, rows32, cols32, colmat,
    s_spec, r_spec, s_coef, r_coef, s_row, r_row, s_col, r_col, local,
):
    w = lax.axis_index("wide")
    n = lax.axis_index("narrow")
    row_at = 2 * lax.rem(n, 8) + lax.div(n, 8)

    barrier = pltpu.get_barrier_semaphore()
    each(1, WIDE, lambda k: pl.semaphore_signal(
        barrier, inc=1, device_id={"wide": wide_step(w, k)}, device_id_type=MESH))
    each(1, NARROW, lambda k: pl.semaphore_signal(
        barrier, inc=1, device_id={"narrow": narrow_step(n, k)}, device_id_type=MESH))

    def spectrum(ch, k):
        d = wide_step(w, k)
        return pltpu.make_async_remote_copy(
            src_ref=spec_out.at[ch, d], dst_ref=spec_in.at[ch, w], send_sem=s_spec.at[ch, k - 1],
            recv_sem=r_spec.at[ch, k - 1], device_id={"wide": d}, device_id_type=MESH,
        )

    def coefficient(ch, k):
        d = narrow_step(n, k)
        return pltpu.make_async_remote_copy(
            src_ref=coef_out.at[ch, d], dst_ref=coef_in.at[ch, n], send_sem=s_coef.at[ch, k - 1],
            recv_sem=r_coef.at[ch, k - 1], device_id={"narrow": d}, device_id_type=MESH,
        )

    def to_wide(offs, source, target, ch, at):
        return [
            pltpu.make_async_remote_copy(
                src_ref=source, dst_ref=target, send_sem=s_col.at[ch, at + i],
                recv_sem=r_col.at[ch, at + i], device_id={"wide": wide_peer(w, off)}, device_id_type=MESH,
            )
            for i, off in enumerate(offs)
        ]

    def to_narrow(offs, source, target, ch, at):
        return [
            pltpu.make_async_remote_copy(
                src_ref=source, dst_ref=target, send_sem=s_row.at[ch, at + i],
                recv_sem=r_row.at[ch, at + i], device_id={"narrow": narrow_peer(n, off)}, device_id_type=MESH,
            )
            for i, off in enumerate(offs)
        ]

    def own_spec(ch):
        return pltpu.make_async_copy(spec_out.at[ch, w], spec_in.at[ch, w], local.at[0, ch])

    def own_coef(ch):
        return pltpu.make_async_copy(coef_out.at[ch, n], coef_in.at[ch, n], local.at[1, ch])

    def own_col(ch):
        return pltpu.make_async_copy(col_out.at[ch], col_in.at[ch, w], local.at[2, ch])

    def own_row(ch):
        return pltpu.make_async_copy(row_out.at[ch], row_in.at[ch, row_at], local.at[3, ch])

    def col_near(ch):
        return to_wide(Z_OFFS, col_out.at[ch], col_in.at[ch, w], ch, 0)

    def row_near(ch):
        return to_narrow(ZLO_OFFS, row_out.at[ch], row_in.at[ch, row_at], ch, 0)

    def col_far(ch):
        block = col_in.at[ch, pl.ds(pl.multiple_of(w - lax.rem(w, 4), 4), 4)]
        return to_wide(Y_OFFS, block, block, ch, len(Z_OFFS))

    def row_far(ch):
        block = row_in.at[ch, pl.ds(pl.multiple_of(2 * lax.rem(n, 8), 2), 2)]
        return to_narrow(XC_OFFS, block, block, ch, len(ZLO_OFFS))

    left = lax.broadcasted_iota(jnp.int32, (ROWS, LANES), 1) < 64
    lane48 = lax.broadcasted_iota(jnp.int32, (2 * ROWS, LANES), 1)
    day = lax.rem(lane48, 64)
    left48 = lane48 < 64

    for slot in (11, 23, 35):
        wave[pl.ds(slot * BAND, BAND), :] = jnp.zeros((BAND, LANES), F32)
    var_ref[...] = jnp.zeros((2 * ROWS, LANES), F32)

    def fourier(ch):
        half = BAND // 2
        mine = order_ref[pl.ds(pl.multiple_of(ch * half, half), half), :]
        hot = (mine == lax.broadcasted_iota(jnp.int32, (half, M), 1)).astype(F32).astype(BF16)
        for c in range(2):
            table[c * half : (c + 1) * half, :] = jnp.dot(
                hot, fourier_ref[c], preferred_element_type=F32
            ).astype(BF16)
        for at, count in ((0, 4), (4, 4), (8, 4), (12, 4), (16, 4), (20, 2)):
            days = x_ref[pl.ds(at, count)].reshape(count * 64, NLON)
            out = lax.dot_general(
                table[...], days, (((1,), (1,)), ((), ())), preferred_element_type=F32
            )
            for i in range(count // 2):
                piece = out[:, i * LANES : (i + 1) * LANES]
                slot = at // 2 + i
                wave[pl.ds(slot * BAND, BAND), :] = piece
                wave[pl.ds((24 + slot) * BAND, BAND), :] = piece
                wave[pl.ds((12 + slot) * BAND, BAND), :] = pltpu.roll(piece, 64, 1)

        def regroup(d):
            blocks = []
            for q in range(2):
                real = wave[pl.ds(d * 2 + q, ROWS, stride=BAND), :]
                imag = wave[pl.ds(12 * BAND + half + d * 2 + q, ROWS, stride=BAND), :]
                blocks.append(jnp.where(left, real, imag))
            spec_out[ch, d] = jnp.concatenate(blocks, axis=0).astype(BF16)

        each(0, WIDE, regroup)

    def send_spectra(ch):
        each(1, WIDE, lambda k: spectrum(ch, k).start())
        own_spec(ch).start()

    def latitude(ch):
        own_spec(ch).wait()
        each(1, WIDE, lambda k: spectrum(ch, k).wait_recv())
        got = spec_in[ch].astype(F32)
        parts = []
        for e in range(2):
            right = got[:, e * ROWS : (e + 1) * ROWS, :].reshape(WIDE * ROWS, LANES).astype(BF16)
            parts.append(jnp.dot(lat_ref[e], right, preferred_element_type=F32))
        for m in range(NARROW):
            both = jnp.concatenate([p[m * ROWS : (m + 1) * ROWS] for p in parts], axis=0)
            coef_out[ch, m] = both.astype(BF16)
        each(1, NARROW, lambda k: coefficient(ch, k).start())
        own_coef(ch).start()

    def residuals(ch):
        own_coef(ch).wait()
        each(1, NARROW, lambda k: coefficient(ch, k).wait_recv())
        lane12 = lax.broadcasted_iota(jnp.int32, (2 * ROWS, 12), 1)
        for i in range(3):
            re = jnp.sum(jnp.where(lane12 == 2 * ch, weight_ref[i], 0.0), axis=1, keepdims=True)
            im = jnp.sum(jnp.where(lane12 == 2 * ch + 1, weight_ref[i], 0.0), axis=1, keepdims=True)
            wexp[i] = jnp.where(left48, re, im)
        before = jnp.zeros((2 * ROWS, LANES), F32)
        total = jnp.zeros((2 * ROWS, LANES), F32)
        held = [None, None]
        for m in range(NARROW):
            now = coef_in[ch, m].astype(F32)
            res = now
            for i in range(3):
                lag = lag_ref[i]
                mixed = jnp.where(day >= 64 - lag, before, now)
                res = res - wexp[i] * pltpu.roll(mixed, lag, 1)
            if m == 0:
                res = jnp.where(day >= LAGMAX, res, 0.0)
            total = total + res * res
            before = pltpu.roll(now, 64, 1)
            for e in range(2):
                top = res[e * ROWS : e * ROWS + 8]
                if m % 2 == 0:
                    held[e] = top
                else:
                    both = jnp.where(left[:8], held[e], pltpu.roll(top, 64, 1))
                    series[pl.ds(e * 64 + (m // 2) * 8, 8), :] = both
        re = jnp.sum(jnp.where(left48, total, 0.0), axis=1, keepdims=True)
        im = jnp.sum(jnp.where(left48, 0.0, total), axis=1, keepdims=True)
        var_ref[...] += jnp.where(lane48 == 2 * ch, re, 0.0) + jnp.where(lane48 == 2 * ch + 1, im, 0.0)
        pieces = [
            series[pl.ds(e * 64 + l, PAIRS, stride=8), :] for e in range(2) for l in range(ROW_DEG)
        ]
        row_out[ch] = jnp.concatenate(pieces, axis=0).astype(BF16)
        pieces = [series[pl.ds(e * 64 + ROW_DEG, PAIRS, stride=8), :] for e in range(2)]
        col_out[ch] = jnp.concatenate(pieces, axis=0).astype(BF16)
        for copy in [own_col(ch), own_row(ch)] + col_near(ch) + row_near(ch):
            copy.start()

    def spread(ch):
        own_col(ch).wait()
        for copy in col_near(ch):
            copy.wait_recv()
        for copy in col_far(ch):
            copy.start()
        own_row(ch).wait()
        for copy in row_near(ch):
            copy.wait_recv()
        for copy in row_far(ch):
            copy.start()

    def within(step, behind, act):
        ch = step - behind

        @pl.when((ch >= 0) & (ch < CH))
        def _():
            act(ch)

    def stage(step):
        within(step, 0, fourier)

        @pl.when(step == 0)
        def _():
            pl.semaphore_wait(barrier, WIDE + NARROW - 2)

        within(step, AHEAD, latitude)
        within(step, 0, send_spectra)
        within(step, AHEAD + 1, residuals)
        within(step, AHEAD + 2, spread)

    each(0, CH + AHEAD + 2, stage)

    def columns(ch):
        for copy in col_far(ch):
            copy.wait_recv()
        for d in range(WIDE):
            cols32[pl.ds(pl.multiple_of((d * 12 + ch * 2) * 8, 8), 16), :] = col_in[ch, d].astype(F32)

    each(0, CH, columns)
    for p in range(PAIRS):
        colmat[:, p * LANES : (p + 1) * LANES] = cols32[pl.ds(p, M, stride=8), :].astype(BF16)

    def panel(ch):
        for copy in row_far(ch):
            copy.wait_recv()
        for m in range(NARROW):
            blk = row_in[ch, 2 * (m % 8) + m // 8].astype(F32)
            for q in range(2):
                rows32[pl.ds(q * 384 + m * 24, 24), :] = blk[q * 24 : q * 24 + 24]
        rows = jnp.concatenate(
            [
                jnp.concatenate([rows32[pl.ds(q * 384 + p, 48, stride=8), :] for p in range(PAIRS)], axis=1)
                for q in range(2)
            ],
            axis=0,
        ).astype(BF16)
        out = lax.dot_general(rows, colmat[...], (((1,), (1,)), ((), ())), preferred_element_type=F32)
        out = out / math.sqrt(NARROW * 64 - LAGMAX)
        for q in range(2):
            panel_ref[ch * 2 + q] = out[q * 48 : q * 48 + 48]

    each(0, CH, panel)
    var_ref[...] = var_ref[...] / (NARROW * 64 - LAGMAX)

    def drain(ch):
        each(1, WIDE, lambda k: spectrum(ch, k).wait_send())
        each(1, NARROW, lambda k: coefficient(ch, k).wait_send())
        for copy in col_near(ch) + col_far(ch) + row_near(ch) + row_far(ch):
            copy.wait_send()

    each(0, CH, drain)


def body(daily_fields, order_table, lag_days, lag_weights):
    fourier = jnp.asarray(fourier_tables(), BF16)
    lat = jnp.asarray(latitude_tables(), BF16)
    x = jnp.transpose(daily_fields, (1, 0, 2))
    order = jnp.transpose(order_table.reshape(WIDE, CH, 2), (1, 0, 2)).reshape(M, 1)
    weights = jnp.transpose(lag_weights.reshape(3, 24, 6, 2, 2), (0, 3, 1, 2, 4)).reshape(3, 48, 12)
    vmem = pl.BlockSpec(memory_space=pltpu.VMEM)
    dma = pltpu.SemaphoreType.DMA
    nw, nn = WIDE - 1, NARROW - 1
    nc, nr = len(Z_OFFS) + len(Y_OFFS), len(ZLO_OFFS) + len(XC_OFFS)
    variance, panel = pl.pallas_call(
        kernel,
        out_shape=(
            jax.ShapeDtypeStruct((2 * ROWS, LANES), F32),
            jax.ShapeDtypeStruct((CH * 2, ROW_DEG * NARROW, M), F32),
        ),
        in_specs=[vmem, pl.BlockSpec(memory_space=pltpu.SMEM), vmem, vmem, vmem, vmem],
        out_specs=(vmem, vmem),
        scratch_shapes=[
            pltpu.VMEM((BAND, NLON), BF16),
            pltpu.VMEM((36 * BAND, LANES), F32),
            pltpu.VMEM((CH, WIDE, 48, LANES), BF16),
            pltpu.VMEM((CH, WIDE, 48, LANES), BF16),
            pltpu.VMEM((CH, NARROW, 48, LANES), BF16),
            pltpu.VMEM((CH, NARROW, 48, LANES), BF16),
            pltpu.VMEM((3, 48, LANES), F32),
            pltpu.VMEM((2 * 64, LANES), F32),
            pltpu.VMEM((CH, 48, LANES), BF16),
            pltpu.VMEM((CH, NARROW, 48, LANES), BF16),
            pltpu.VMEM((CH, 16, LANES), BF16),
            pltpu.VMEM((CH, WIDE, 16, LANES), BF16),
            pltpu.VMEM((2 * 384, LANES), F32),
            pltpu.VMEM((M * 8, LANES), F32),
            pltpu.VMEM((M, PAIRS * LANES), BF16),
            dma((CH, nw)), dma((CH, nw)), dma((CH, nn)), dma((CH, nn)),
            dma((CH, nr)), dma((CH, nr)), dma((CH, nc)), dma((CH, nc)), dma((4, CH)),
        ],
        compiler_params=pltpu.CompilerParams(
            collective_id=0, has_side_effects=True, vmem_limit_bytes=60 * 1024 * 1024
        ),
        name="sphere",
    )(order, lag_days, weights, fourier, lat, x)
    noise = jnp.transpose(variance[:, :12].reshape(2, 24, 6, 2), (1, 2, 0, 3)).reshape(24, 12, 2)
    return noise, panel


def solution(mesh):
    placed = (P("narrow", "wide", None), P(), P(), P(None, "narrow", "wide", None))
    return jax.shard_map(
        body,
        mesh=mesh,
        in_specs=placed,
        out_specs=(P("narrow", "wide", None), P("wide", None, "narrow")),
        check_vma=False,
    )
```

time: 135 us -> 128 us (0.948)
  Pallas kernels: 127 us -> 121 us
    pallas_call x1, Pallas kernels: 127 us -> 121 us  [body(): pl.pallas_call(kernel, out_shape=(jax.ShapeDtypeStruct((2 * ROWS, LANES),...]
where the time goes in v2:
time: 128 us
  Pallas kernels  121 us (95%)
  local copies, waits for them, and re-layouts  6.85 us (5%)
    pallas_call x1, Pallas kernels, body(): pl.pallas_call(kernel, out_shape=(jax.ShapeDtypeStruct((2 * ROWS, LANES),...  121 us

profile of v2, /device:TPU:1, one launch (start us, length us, event | category | flops | bytes accessed | tf_op | source)
XLA Modules:
  0.0 128.1 jit_solution(377327191205985314)
XLA Ops:
  0.6 0.8 copy.22
  1.4 0.1 reshape.25
  1.5 0.7 copy.18.weight_ref
  2.2 0.8 reshape.22
  3.1 0.8 reshape.28.order_ref
  3.9 120.6 %sphere.1 = (f32[48,128]{1,0:T(8,128)}, f32[12,48,384]{2,1,0:T(8,128)}) custom-call(s32[384,1]{1,0:T(8,128)} %reshape.28.order_ref, s32[3]{0:T(128)} %lag_ref.1, f32[3,48,12]{2,1,0:T(8,128)} %copy.18.weight_ref, bf16[2,384,1440]{2,1,0:T(8,128)(2,1)} %constant.4.clone.fourier_ref, bf16[2,384,768]{2,1,0:T(8,128)(2,1)} %constant.5.clone.lat_ref, ...), custom_call_target="tpu_custom_call" | custom-call | tf_op jit(solution)/shard_map/sphere/pallas_call | solution.py:349
  124.5 0.8 copy.19
  125.3 0.1 reshape.26
  125.4 0.6 copy.20
  126.0 2.1 %copy.24 = f32[12,48,384]{2,1,0:T(8,128)} copy(f32[12,48,384]{2,1,0:T(8,128)} %get-tuple-element.9) | data formatting | bytes 1769472
  (1 shorter events, 0.0 us)
